TPU v7x, 512 devices: a whole 4x8x8 slice. The times are simulated.
512 devices in a mesh: dom: 16 (over y, core), aux: 32 (over x, z).
Axes of the slice: x: 4, y: 8, z: 8, core: 2. Of those that a mesh axis runs over, the one named last changes fastest.
Arguments:
- integrals: bfloat16 [16, 1024, 512, 128], P('dom', 'aux'), may hold values from -0.25 to 0.25
- density: bfloat16 [16, 4, 128, 128], P('dom'), may hold values from -0.25 to 0.25
- dens_cols: int32 [16, 4], replicated, may hold values from 0 to 15, as said below
- neighbours: int32 [16, 4], replicated, may hold values from 0 to 15, as said below
- metric: bfloat16 [16, 1024, 1024], P('dom', 'aux'), may hold values from -0.5 to 2.5, as said below
Outputs:
- exchange: float32 [16, 128, 128], P('dom')
Inputs may be any that keep to these rules, and one draw needn't show every extreme that they name: `neighbours`: in each row the entries are distinct; position 0 holds the row's own block, the others are blocks within cyclic distance 2 of it, both blocks at distance 1 among them. `dens_cols`: in each row the entries are distinct; position 0 holds the row's own block, the others are blocks within cyclic distance 2 of it, both blocks at distance 1 among them. `metric`: each domain's matrix is symmetric.
All inputs are finite; a program needn't handle non-finite values.
Results may differ from a plain program's by a relative error of at most 0.004.
Values may be sent and summed in bfloat16 or wider, within the bound.
No kernel may reach another device: no remote copies, remote signals or barrier semaphores. Data moves between devices by JAX's collectives and lax.ppermute only.
A program may use at most 64 MiB of HBM per device.

v0:
```python
import jax
import jax.numpy as jnp
from jax import lax
from jax.sharding import PartitionSpec as P

RAD = 2


def passed_along(block, axis, distance):
    devices = range(lax.axis_size(axis))
    route = [((i - distance) % len(devices), i) for i in devices]
    return lax.ppermute(block, axis, route)


def body(integrals, density, dens_cols, neighbours, metric):
    domain_count = lax.axis_size("dom")
    my_domain = lax.axis_index("dom")
    block_size = density.shape[2]
    neigh_count = neighbours.shape[1]
    my_blocks = lax.dynamic_index_in_dim(neighbours, my_domain, 0, keepdims=False)
    slab_list = []
    for offset in range(-RAD, RAD + 1):
        if offset == 0:
            slab_list.append(density[0])
        else:
            slab_list.append(passed_along(density, "dom", -offset)[0])
    row_slabs = jnp.stack(slab_list)
    slot_index = (my_blocks - my_domain + RAD) % domain_count
    picked = jnp.take(row_slabs, slot_index, axis=0)
    tile_cols = jnp.take(dens_cols, my_blocks, axis=0)
    matches = (tile_cols[:, None, :] == my_blocks[None, :, None]).astype(jnp.bfloat16)
    dense_tiles = jnp.einsum("jsk,jkab->jasb", matches, picked, preferred_element_type=jnp.float32)
    density_local = dense_tiles.astype(jnp.bfloat16).reshape(
        neigh_count * block_size, neigh_count * block_size
    )
    half_product = jnp.einsum(
        "ls,plm->psm", density_local, integrals[0], preferred_element_type=jnp.float32
    ).astype(jnp.bfloat16)
    half_moved, ints_moved = (
        lax.all_to_all(half_product[None], "aux", split_axis=2, concat_axis=1, tiled=True),
        lax.all_to_all(integrals, "aux", split_axis=2, concat_axis=1, tiled=True),
    )
    columns = ints_moved[0].reshape(ints_moved.shape[1], -1)
    fitted = jnp.dot(
        lax.all_gather(metric, "aux", axis=1, tiled=True)[0],
        columns,
        preferred_element_type=jnp.float32,
    ).astype(jnp.bfloat16)
    fitted = fitted.reshape(half_moved.shape[1:])
    partial_value = jnp.einsum(
        "psm,psn->mn", half_moved[0], fitted, preferred_element_type=jnp.float32
    )
    summed = lax.psum(partial_value, "aux")
    return summed[None]


def solution(mesh):
    return jax.shard_map(
        body,
        mesh=mesh,
        in_specs=(
            P("dom", "aux", None, None),
            P("dom", None, None, None),
            P(),
            P(),
            P("dom", "aux", None),
        ),
        out_specs=P("dom", None, None),
        check_vma=False,
    )
```

profile of v0, /device:TPU:2, one launch (start us, length us, event | category | flops | bytes accessed | tf_op | source)
XLA Modules:
  0.0 421.5 jit_solution(17828483009210059733)
XLA Ops:
  6.5 0.0 copy-start
  6.5 6.9 %copy.30 = bf16[1,32,512,128]{3,1,0,2:T(8,128)(2,1)} copy(bf16[1,32,512,128]{3,2,1,0:T(8,128)(2,1)} %param.5) | data formatting | bytes 8388608 | tf_op args[0]
  13.4 0.0 copy-start.2
  13.4 0.0 copy-start.3
  13.4 13.7 %all-to-all-start.1 = ((bf16[1,32,512,128]{3,1,0,2:T(8,128)(2,1)}), bf16[1,32,512,128]{3,1,0,2:T(8,128)(2,1)}, u32[]{:S(2)}, u32[]{:S(2)}) async-start(bf16[1,32,512,128]{3,1,0,2:T(8,128)(2,1)} %copy.30), calls=%async_computation.1 | async-start | bytes 8388608 | tf_op jit(solution)/shard_map/all_to_all | solution.py:41
  27.1 0.0 copy-done.2
  27.1 3.5 collective-permute-start
  30.6 0.0 collective-permute-start.1
  30.6 2.9 collective-permute-start.2
  33.5 2.6 collective-permute-start.3
  36.1 0.0 copy-done.3
  36.2 0.1 copy.24
  36.2 0.0 copy-done
  36.2 0.2 dynamic-slice_reduce_fusion
  36.5 0.6 gather_fusion.1
  37.0 0.1 broadcast_select_fusion.1
  37.1 0.0 collective-permute-done
  37.1 0.0 collective-permute-done.1
  37.2 0.0 collective-permute-done.2
  37.2 3.2 collective-permute-done.3
  40.4 0.6 gather_fusion
  41.1 0.1 broadcast_select_fusion
  41.2 0.5 convolution_convert_fusion
  41.8 4.6 %convert_bitcast_fusion.1 = bf16[1,32,512,128]{3,2,1,0:T(8,128)(2,1)S(1)} fusion(bf16[1,32,512,128]{3,2,1,0:T(8,128)(2,1)} %param.5, bf16[64,8,4,128]{3,2,1,0:T(4,128)(2,1)S(1)} %bitcast.62), kind=kOutput, calls=%fused_computation.8 | convolution fusion | flops 2149580800 | bytes 8912896 | tf_op jit(solution)/shard_map/ls,plm->psm/dot_general | solution.py:36
  46.3 4.6 %copy.27 = bf16[1,32,512,128]{3,1,0,2:T(8,128)(2,1)} copy(bf16[1,32,512,128]{3,2,1,0:T(8,128)(2,1)S(1)} %convert_bitcast_fusion.1) | data formatting | bytes 8388608 | tf_op jit(solution)/shard_map/broadcast_in_dim | solution.py:40
  51.0 70.6 %all-to-all-done.1 = bf16[1,32,512,128]{3,1,0,2:T(8,128)(2,1)} async-done(((bf16[1,32,512,128]{3,1,0,2:T(8,128)(2,1)}), bf16[1,32,512,128]{3,1,0,2:T(8,128)(2,1)}, u32[]{:S(2)}, u32[]{:S(2)}) %all-to-all-start.1) | async-done | bytes 4194336 | tf_op jit(solution)/shard_map/all_to_all | solution.py:41
  121.6 7.6 %all-to-all-start = ((bf16[1,32,512,128]{3,1,0,2:T(8,128)(2,1)}), bf16[1,32,512,128]{3,1,0,2:T(8,128)(2,1)}, u32[]{:S(2)}, u32[]{:S(2)}) async-start(bf16[1,32,512,128]{3,1,0,2:T(8,128)(2,1)} %copy.27), calls=%async_computation | async-start | bytes 8388608 | tf_op jit(solution)/shard_map/all_to_all | solution.py:40
  129.2 0.0 all-gather.2.cloned.1.call-start
  129.2 0.7 all-gather.2.cloned.1.call-update
  129.9 0.2 all-reduce.2.cloned.1.call-start
  130.1 6.1 %copy.31 = bf16[1,32,32,16,128]{4,3,1,2,0:T(8,128)(2,1)} copy(bf16[1,32,32,16,128]{4,1,3,2,0:T(8,128)(2,1)} %bitcast.13) | data formatting | bytes 8388608 | tf_op jit(solution)/shard_map/all_to_all | solution.py:41
  136.2 106.2 %all-gather.2.cloned.1.call-done = bf16[1,1024,1024]{2,1,0:T(8,128)(2,1)} async-done(((bf16[1,32,1024]{2,1,0:T(8,128)(2,1)}), bf16[1,1024,1024]{2,1,0:T(8,128)(2,1)}) %all-gather.2.cloned.1.call-update) | async-done | bytes 2097168 | tf_op jit(solution)/shard_map/all_gather | solution.py:45
  242.4 7.3 %convert_bitcast_fusion = bf16[128,8,16,128]{3,1,2,0:T(8,128)(2,1)S(1)} fusion(bf16[128,8,16,128]{3,2,1,0:T(8,128)(2,1)} %bitcast.60, bf16[1,1024,1024]{2,1,0:T(8,128)(2,1)} %all-gather.2.cloned.1.call-done), kind=kOutput, calls=%fused_computation.7 | convolution fusion | flops 4297064448 | bytes 10485760 | tf_op jit(solution)/shard_map/dot_general | solution.py:44
  249.8 3.4 copy.37
  253.1 0.0 all-to-all-done
  253.1 3.8 copy.28
  257.0 0.0 copy-start.1
  257.0 1.2 copy.29
  258.1 1.0 copy-done.1
  259.1 1.9 convolution_bitcast_fusion
  261.1 0.0 all-reduce.2.cloned.1.call-update
  261.1 152.0 %all-reduce.2.cloned.1.call-done = f32[1,128,128]{2,1,0:T(8,128)} async-done(((f32[1,128,128]{2,1,0:T(8,128)}), f32[1,128,128]{2,1,0:T(8,128)}) %all-reduce.2.cloned.1.call-update) | async-done | bytes 65552 | tf_op jit(solution)/shard_map/psum | solution.py:53
  413.1 1.5 copy.55
  (9 shorter events, 0.1 us)
Async XLA Ops:
  6.5 29.7 %copy-start = (s32[16,4]{0,1:T(4,128)S(1)}, s32[16,4]{0,1:T(4,128)}, u32[]{:S(2)}) copy-start(s32[16,4]{0,1:T(4,128)} %param.8) | copy-start | bytes 772
  13.4 13.7 %copy-start.2 = (bf16[1,4,128,128]{3,2,1,0:T(8,128)(2,1)S(1)}, bf16[1,4,128,128]{3,2,1,0:T(8,128)(2,1)}, u32[]{:S(2)}) copy-start(bf16[1,4,128,128]{3,2,1,0:T(8,128)(2,1)} %param.6) | copy-start | bytes 393220
  13.4 22.7 %copy-start.3 = (s32[16,4]{0,1:T(4,128)S(1)}, s32[16,4]{0,1:T(4,128)}, u32[]{:S(2)}) copy-start(s32[16,4]{0,1:T(4,128)} %param.7) | copy-start | bytes 772
  13.4 108.2 %all-to-all-start.1 = ((bf16[1,32,512,128]{3,1,0,2:T(8,128)(2,1)}), bf16[1,32,512,128]{3,1,0,2:T(8,128)(2,1)}, u32[]{:S(2)}, u32[]{:S(2)}) async-start(bf16[1,32,512,128]{3,1,0,2:T(8,128)(2,1)} %copy.30), calls=%async_computation.1 | async-start | bytes 8388608 | tf_op jit(solution)/shard_map/all_to_all | solution.py:41
  27.1 10.0 %collective-permute-start = (bf16[1,4,128,128]{3,2,1,0:T(8,128)(2,1)S(1)}, bf16[1,4,128,128]{3,2,1,0:T(8,128)(2,1)S(1)}, u32[]{:S(2)}, u32[]{:S(2)}) collective-permute-start(bf16[1,4,128,128]{3,2,1,0:T(8,128)(2,1)S(1)} %copy-done.2), channel_id=1, source_target_pairs={{448,0},{480,32},{0,64},{32,96},{64,128},{96,160},{128,192},{160,2... | collective-permute-start | bytes 393224 | tf_op jit(solution)/shard_map/ppermute | solution.py:12
  30.6 6.6 %collective-permute-start.1 = (bf16[1,4,128,128]{3,2,1,0:T(8,128)(2,1)S(1)}, bf16[1,4,128,128]{3,2,1,0:T(8,128)(2,1)S(1)}, u32[]{:S(2)}, u32[]{:S(2)}) collective-permute-start(bf16[1,4,128,128]{3,2,1,0:T(8,128)(2,1)S(1)} %copy-done.2), channel_id=1, source_target_pairs={{480,0},{0,32},{32,64},{64,96},{96,128},{128,160},{160,192},{192,2... | collective-permute-start | bytes 393224 | tf_op jit(solution)/shard_map/ppermute | solution.py:12
  30.6 6.6 %collective-permute-start.2 = (bf16[1,4,128,128]{3,2,1,0:T(8,128)(2,1)S(1)}, bf16[1,4,128,128]{3,2,1,0:T(8,128)(2,1)S(1)}, u32[]{:S(2)}, u32[]{:S(2)}) collective-permute-start(bf16[1,4,128,128]{3,2,1,0:T(8,128)(2,1)S(1)} %copy-done.2), channel_id=1, source_target_pairs={{32,0},{64,32},{96,64},{128,96},{160,128},{192,160},{224,192},{256... | collective-permute-start | bytes 393224 | tf_op jit(solution)/shard_map/ppermute | solution.py:12
  33.5 6.8 %collective-permute-start.3 = (bf16[1,4,128,128]{3,2,1,0:T(8,128)(2,1)S(1)}, bf16[1,4,128,128]{3,2,1,0:T(8,128)(2,1)S(1)}, u32[]{:S(2)}, u32[]{:S(2)}) collective-permute-start(bf16[1,4,128,128]{3,2,1,0:T(8,128)(2,1)S(1)} %copy-done.2), channel_id=1, source_target_pairs={{64,0},{96,32},{128,64},{160,96},{192,128},{224,160},{256,192},{28... | collective-permute-start | bytes 393224 | tf_op jit(solution)/shard_map/ppermute | solution.py:12
  121.6 131.6 %all-to-all-start = ((bf16[1,32,512,128]{3,1,0,2:T(8,128)(2,1)}), bf16[1,32,512,128]{3,1,0,2:T(8,128)(2,1)}, u32[]{:S(2)}, u32[]{:S(2)}) async-start(bf16[1,32,512,128]{3,1,0,2:T(8,128)(2,1)} %copy.27), calls=%async_computation | async-start | bytes 8388608 | tf_op jit(solution)/shard_map/all_to_all | solution.py:40
  129.2 113.3 %all-gather.2.cloned.1.call-start = ((), (), s32[]{:S(2)}) async-start(), calls=%async_computation.2 | async-start | bytes 2162688 | tf_op jit(solution)/shard_map/all_gather | solution.py:45
  129.9 283.2 %all-reduce.2.cloned.1.call-start = ((), (), s32[]{:S(2)}) async-start(), calls=%async_computation.3 | async-start | bytes 131072 | tf_op jit(solution)/shard_map/psum | solution.py:53
  257.0 2.2 copy-start.1
Sparse Core Ops, SparseCore 0:
  133.1 109.2 all-gather.1
  261.2 151.8 all-reduce.1
where the time goes:
time: 422 us; the launch traced here: 421 us
  waiting for transfers between devices  333 us (79%)
  starting transfers between devices  30.5 us (7%)
  local copies, waits for them, and re-layouts  30 us (7%)
  matrix products  14.4 us (3%)
  between operations  13.6 us (3%)
    psum x1, waiting for transfers between devices, body(): summed = lax.psum(partial_value, 'aux')  152 us
    all_gather x1, waiting for transfers between devices, body(): lax.all_gather(metric, 'aux', axis=1, tiled=True)[0]  106 us
    all_to_all x1, waiting for transfers between devices, body(): lax.all_to_all(integrals, 'aux', split_axis=2, concat_axis=1, tiled=True)  70.6 us
    all_to_all x1, starting transfers between devices, body(): lax.all_to_all(integrals, 'aux', split_axis=2, concat_axis=1, tiled=True)  13.7 us
    unnamed x16, local copies, waits for them, and re-layouts  12.9 us
    ppermute x4, starting transfers between devices, passed_along(): return lax.ppermute(block, axis, route)  9.04 us
  transfers between devices with their start and end apart: 8, of which 4 were waited for; matrix products, arithmetic and copies ran while one was open for 7% of the time, Pallas kernels for 0%

commit v1 on v0

--- a/solution.py
+++ b/solution.py
@@ -50,7 +50,7 @@
     partial_value = jnp.einsum(
         "psm,psn->mn", half_moved[0], fitted, preferred_element_type=jnp.float32
     )
-    summed = lax.psum(partial_value, "aux")
+    summed = jnp.sum(lax.all_gather(partial_value, "aux"), axis=0)
     return summed[None]
 
 

time: 422 us -> 354 us (0.84)
  the two profiles are of different devices: /device:TPU:2 before, /device:TPU:8 now
where the time goes in v1:
time: 354 us; the launch traced here: 353 us
  waiting for transfers between devices  267 us (75%)
  local copies, waits for them, and re-layouts  28.5 us (8%)
  starting transfers between devices  27.6 us (8%)
  matrix products  14.4 us (4%)
  between operations  13.6 us (4%)
    all_gather x1, waiting for transfers between devices, body(): lax.all_gather(metric, 'aux', axis=1, tiled=True)[0]  107 us
    all_gather x1, waiting for transfers between devices, body(): summed = jnp.sum(lax.all_gather(partial_value, 'aux'), axis=0)  82.5 us
    all_to_all x1, waiting for transfers between devices, body(): lax.all_to_all(integrals, 'aux', split_axis=2, concat_axis=1, tiled=True)  72.9 us
    all_to_all x1, starting transfers between devices, body(): lax.all_to_all(integrals, 'aux', split_axis=2, concat_axis=1, tiled=True)  13.4 us
    unnamed x15, local copies, waits for them, and re-layouts  11.4 us
    ppermute x4, starting transfers between devices, passed_along(): return lax.ppermute(block, axis, route)  8.79 us
    dot_general x1, matrix products, body(): jnp.dot(lax.all_gather(metric, 'aux', axis=1, tiled=True)[0], columns, pr...  7.32 us
  transfers between devices with their start and end apart: 8, of which 4 were waited for; matrix products, arithmetic and copies ran while one was open for 8% of the time, Pallas kernels for 0%

profile of v1, /device:TPU:8, one launch (start us, length us, event | category | flops | bytes accessed | tf_op | source)
XLA Modules:
  0.0 353.3 jit_solution(2800287532996315340)
XLA Ops:
  6.5 0.0 copy-start
  6.5 6.9 %copy.30 = bf16[1,32,512,128]{3,1,0,2:T(8,128)(2,1)} copy(bf16[1,32,512,128]{3,2,1,0:T(8,128)(2,1)} %param.5) | data formatting | bytes 8388608 | tf_op args[0]
  13.4 0.0 copy-start.2
  13.4 0.0 copy-start.3
  13.4 13.4 %all-to-all-start.1 = ((bf16[1,32,512,128]{3,1,0,2:T(8,128)(2,1)}), bf16[1,32,512,128]{3,1,0,2:T(8,128)(2,1)}, u32[]{:S(2)}, u32[]{:S(2)}) async-start(bf16[1,32,512,128]{3,1,0,2:T(8,128)(2,1)} %copy.30), calls=%async_computation.1 | async-start | bytes 8388608 | tf_op jit(solution)/shard_map/all_to_all | solution.py:41
  26.8 0.0 copy-done.2
  26.9 3.5 collective-permute-start
  30.3 0.0 collective-permute-start.1
  30.4 1.7 collective-permute-start.2
  32.1 3.6 %collective-permute-start.3 = (bf16[1,4,128,128]{3,2,1,0:T(8,128)(2,1)S(1)}, bf16[1,4,128,128]{3,2,1,0:T(8,128)(2,1)S(1)}, u32[]{:S(2)}, u32[]{:S(2)}) collective-permute-start(bf16[1,4,128,128]{3,2,1,0:T(8,128)(2,1)S(1)} %copy-done.2), channel_id=1, source_target_pairs={{64,0},{96,32},{128,64},{160,96},{192,128},{224,160},{256,192},{28... | collective-permute-start | bytes 393224 | tf_op jit(solution)/shard_map/ppermute | solution.py:12
  35.7 0.0 copy-done.3
  35.7 0.1 copy.24
  35.8 0.0 copy-done
  35.8 0.2 dynamic-slice_reduce_fusion
  36.0 0.6 gather_fusion.1
  36.6 0.1 broadcast_select_fusion.1
  36.6 0.0 collective-permute-done
  36.7 0.0 collective-permute-done.1
  36.7 0.0 collective-permute-done.2
  36.8 3.6 %collective-permute-done.3 = bf16[1,4,128,128]{3,2,1,0:T(8,128)(2,1)S(1)} collective-permute-done((bf16[1,4,128,128]{3,2,1,0:T(8,128)(2,1)S(1)}, bf16[1,4,128,128]{3,2,1,0:T(8,128)(2,1)S(1)}, u32[]{:S(2)}, u32[]{:S(2)}) %collective-permute-start.3) | collective-permute-done | bytes 131104 | tf_op jit(solution)/shard_map/ppermute | solution.py:12
  40.4 0.6 gather_fusion
  41.0 0.1 broadcast_select_fusion
  41.1 0.5 convolution_convert_fusion
  41.7 4.6 %convert_bitcast_fusion.1 = bf16[1,32,512,128]{3,2,1,0:T(8,128)(2,1)S(1)} fusion(bf16[1,32,512,128]{3,2,1,0:T(8,128)(2,1)} %param.5, bf16[64,8,4,128]{3,2,1,0:T(4,128)(2,1)S(1)} %bitcast.64), kind=kOutput, calls=%fused_computation.8 | convolution fusion | flops 2149580800 | bytes 8912896 | tf_op jit(solution)/shard_map/ls,plm->psm/dot_general | solution.py:36
  46.3 4.6 %copy.27 = bf16[1,32,512,128]{3,1,0,2:T(8,128)(2,1)} copy(bf16[1,32,512,128]{3,2,1,0:T(8,128)(2,1)S(1)} %convert_bitcast_fusion.1) | data formatting | bytes 8388608 | tf_op jit(solution)/shard_map/broadcast_in_dim | solution.py:40
  50.9 72.9 %all-to-all-done.1 = bf16[1,32,512,128]{3,1,0,2:T(8,128)(2,1)} async-done(((bf16[1,32,512,128]{3,1,0,2:T(8,128)(2,1)}), bf16[1,32,512,128]{3,1,0,2:T(8,128)(2,1)}, u32[]{:S(2)}, u32[]{:S(2)}) %all-to-all-start.1) | async-done | bytes 4194336 | tf_op jit(solution)/shard_map/all_to_all | solution.py:41
  123.8 5.1 %all-to-all-start = ((bf16[1,32,512,128]{3,1,0,2:T(8,128)(2,1)}), bf16[1,32,512,128]{3,1,0,2:T(8,128)(2,1)}, u32[]{:S(2)}, u32[]{:S(2)}) async-start(bf16[1,32,512,128]{3,1,0,2:T(8,128)(2,1)} %copy.27), calls=%async_computation | async-start | bytes 8388608 | tf_op jit(solution)/shard_map/all_to_all | solution.py:40
  128.9 0.0 all-gather.4.cloned.1.call-start
  129.0 0.7 all-gather.4.cloned.1.call-update
  129.7 0.2 all-gather.6.cloned.1.call-start
  129.9 6.1 %copy.31 = bf16[1,32,32,16,128]{4,3,1,2,0:T(8,128)(2,1)} copy(bf16[1,32,32,16,128]{4,1,3,2,0:T(8,128)(2,1)} %bitcast.13) | data formatting | bytes 8388608 | tf_op jit(solution)/shard_map/all_to_all | solution.py:41
  136.0 107.0 %all-gather.4.cloned.1.call-done = bf16[1,1024,1024]{2,1,0:T(8,128)(2,1)} async-done(((bf16[1,32,1024]{2,1,0:T(8,128)(2,1)}), bf16[1,1024,1024]{2,1,0:T(8,128)(2,1)}) %all-gather.4.cloned.1.call-update) | async-done | bytes 2097168 | tf_op jit(solution)/shard_map/all_gather | solution.py:45
  243.0 7.3 %convert_bitcast_fusion = bf16[128,8,16,128]{3,1,2,0:T(8,128)(2,1)S(1)} fusion(bf16[128,8,16,128]{3,2,1,0:T(8,128)(2,1)} %bitcast.61, bf16[1,1024,1024]{2,1,0:T(8,128)(2,1)} %all-gather.4.cloned.1.call-done), kind=kOutput, calls=%fused_computation.7 | convolution fusion | flops 4297064448 | bytes 10485760 | tf_op jit(solution)/shard_map/dot_general | solution.py:44
  250.3 3.4 copy.37
  253.7 0.0 all-to-all-done
  253.7 3.8 %copy.28 = bf16[1,32,512,128]{3,2,1,0:T(8,128)(2,1)S(1)} copy(bf16[1,32,512,128]{3,1,0,2:T(8,128)(2,1)} %all-to-all-done) | data formatting | bytes 8388608 | tf_op jit(solution)/shard_map/all_to_all | solution.py:40
  257.5 0.0 copy-start.1
  257.5 1.2 copy.29
  258.7 1.0 copy-done.1
  259.7 1.9 convolution_bitcast_fusion
  261.6 0.0 all-gather.6.cloned.1.call-update
  261.6 82.5 %all-gather.6.cloned.1.call-done = f32[4096,128]{1,0:T(8,128)} async-done(((f32[128,128]{1,0:T(8,128)}), f32[4096,128]{1,0:T(8,128)}) %all-gather.6.cloned.1.call-update) | async-done | bytes 2097168 | tf_op jit(solution)/shard_map/all_gather | solution.py:53
  344.1 2.3 reduce_sum.9
  (9 shorter events, 0.1 us)
Async XLA Ops:
  6.5 29.2 %copy-start = (s32[16,4]{0,1:T(4,128)S(1)}, s32[16,4]{0,1:T(4,128)}, u32[]{:S(2)}) copy-start(s32[16,4]{0,1:T(4,128)} %param.8) | copy-start | bytes 772
  13.4 13.4 %copy-start.2 = (bf16[1,4,128,128]{3,2,1,0:T(8,128)(2,1)S(1)}, bf16[1,4,128,128]{3,2,1,0:T(8,128)(2,1)}, u32[]{:S(2)}) copy-start(bf16[1,4,128,128]{3,2,1,0:T(8,128)(2,1)} %param.6) | copy-start | bytes 393220
  13.4 22.3 %copy-start.3 = (s32[16,4]{0,1:T(4,128)S(1)}, s32[16,4]{0,1:T(4,128)}, u32[]{:S(2)}) copy-start(s32[16,4]{0,1:T(4,128)} %param.7) | copy-start | bytes 772
  13.4 110.4 %all-to-all-start.1 = ((bf16[1,32,512,128]{3,1,0,2:T(8,128)(2,1)}), bf16[1,32,512,128]{3,1,0,2:T(8,128)(2,1)}, u32[]{:S(2)}, u32[]{:S(2)}) async-start(bf16[1,32,512,128]{3,1,0,2:T(8,128)(2,1)} %copy.30), calls=%async_computation.1 | async-start | bytes 8388608 | tf_op jit(solution)/shard_map/all_to_all | solution.py:41
  26.9 9.8 %collective-permute-start = (bf16[1,4,128,128]{3,2,1,0:T(8,128)(2,1)S(1)}, bf16[1,4,128,128]{3,2,1,0:T(8,128)(2,1)S(1)}, u32[]{:S(2)}, u32[]{:S(2)}) collective-permute-start(bf16[1,4,128,128]{3,2,1,0:T(8,128)(2,1)S(1)} %copy-done.2), channel_id=1, source_target_pairs={{448,0},{480,32},{0,64},{32,96},{64,128},{96,160},{128,192},{160,2... | collective-permute-start | bytes 393224 | tf_op jit(solution)/shard_map/ppermute | solution.py:12
  30.3 6.3 %collective-permute-start.1 = (bf16[1,4,128,128]{3,2,1,0:T(8,128)(2,1)S(1)}, bf16[1,4,128,128]{3,2,1,0:T(8,128)(2,1)S(1)}, u32[]{:S(2)}, u32[]{:S(2)}) collective-permute-start(bf16[1,4,128,128]{3,2,1,0:T(8,128)(2,1)S(1)} %copy-done.2), channel_id=1, source_target_pairs={{480,0},{0,32},{32,64},{64,96},{96,128},{128,160},{160,192},{192,2... | collective-permute-start | bytes 393224 | tf_op jit(solution)/shard_map/ppermute | solution.py:12
  30.4 6.4 %collective-permute-start.2 = (bf16[1,4,128,128]{3,2,1,0:T(8,128)(2,1)S(1)}, bf16[1,4,128,128]{3,2,1,0:T(8,128)(2,1)S(1)}, u32[]{:S(2)}, u32[]{:S(2)}) collective-permute-start(bf16[1,4,128,128]{3,2,1,0:T(8,128)(2,1)S(1)} %copy-done.2), channel_id=1, source_target_pairs={{32,0},{64,32},{96,64},{128,96},{160,128},{192,160},{224,192},{256... | collective-permute-start | bytes 393224 | tf_op jit(solution)/shard_map/ppermute | solution.py:12
  32.1 8.2 %collective-permute-start.3 = (bf16[1,4,128,128]{3,2,1,0:T(8,128)(2,1)S(1)}, bf16[1,4,128,128]{3,2,1,0:T(8,128)(2,1)S(1)}, u32[]{:S(2)}, u32[]{:S(2)}) collective-permute-start(bf16[1,4,128,128]{3,2,1,0:T(8,128)(2,1)S(1)} %copy-done.2), channel_id=1, source_target_pairs={{64,0},{96,32},{128,64},{160,96},{192,128},{224,160},{256,192},{28... | collective-permute-start | bytes 393224 | tf_op jit(solution)/shard_map/ppermute | solution.py:12
  123.8 129.8 %all-to-all-start = ((bf16[1,32,512,128]{3,1,0,2:T(8,128)(2,1)}), bf16[1,32,512,128]{3,1,0,2:T(8,128)(2,1)}, u32[]{:S(2)}, u32[]{:S(2)}) async-start(bf16[1,32,512,128]{3,1,0,2:T(8,128)(2,1)} %copy.27), calls=%async_computation | async-start | bytes 8388608 | tf_op jit(solution)/shard_map/all_to_all | solution.py:40
  128.9 114.0 %all-gather.4.cloned.1.call-start = ((), (), s32[]{:S(2)}) async-start(), calls=%async_computation.2 | async-start | bytes 2162688 | tf_op jit(solution)/shard_map/all_gather | solution.py:45
  129.7 214.4 %all-gather.6.cloned.1.call-start = ((), (), s32[]{:S(2)}) async-start(), calls=%async_computation.3 | async-start | bytes 2162688 | tf_op jit(solution)/shard_map/all_gather | solution.py:53
  257.5 2.2 copy-start.1
Sparse Core Ops, SparseCore 0:
  132.9 110.0 all-gather.3
  261.8 82.3 all-gather.5
